TPU v7x, 128 devices: a whole 4x4x4 slice. The times are simulated.
128 devices in a mesh: shard: 16 (over y, z), tensor: 4 (over x), section: 2 (over core).
Axes of the slice: x: 4, y: 4, z: 4, core: 2. Of those that a mesh axis runs over, the one named last changes fastest.
Arguments:
- attention_grads: float32 [16, 4, 768, 768], P('shard', 'section', 'tensor'), may hold values from -48 to 48
- feedforward_grads: float32 [16, 2, 3072, 768], P('shard', 'section', 'tensor'), may hold values from -48 to 48
- attention_errors: float32 [16, 4, 768, 768], P('shard', 'section', 'tensor'), may hold values from -3 to 3
- feedforward_errors: float32 [16, 2, 3072, 768], P('shard', 'section', 'tensor'), may hold values from -3 to 3
- attention_factor: float32 [4, 768, 32], P('section'), may hold values from -0.21875 to 0.21875
- feedforward_factor: float32 [2, 768, 32], P('section'), may hold values from -0.21875 to 0.21875
- attention_momentum: float32 [4, 768, 768], P('section', 'tensor', 'shard'), may hold values from -3 to 3
- feedforward_momentum: float32 [2, 3072, 768], P('section', 'tensor', 'shard'), may hold values from -3 to 3
- attention_master: float32 [4, 768, 768], P('section', 'tensor', 'shard'), may hold values from -3 to 3
- feedforward_master: float32 [2, 3072, 768], P('section', 'tensor', 'shard'), may hold values from -3 to 3
- gain_grads: float32 [16, 2, 768], P('shard', 'section', 'tensor'), may hold values from -6 to 6
- bias_grads: float32 [16, 12, 32], P('shard', 'tensor'), may hold values from -6 to 6
- gain_momentum: float32 [2, 768], P('section', 'tensor'), may hold values from -3 to 3
- gain_weight: float32 [2, 768], P('section', 'tensor'), may hold values from 0.5 to 1.5
- bias_momentum: float32 [12, 32], P('tensor'), may hold values from -3 to 3
- bias_weight: float32 [12, 32], P('tensor'), may hold values from -4 to 4
Outputs:
- attention_errors_new: float32 [16, 4, 768, 768], P('shard', 'section', 'tensor')
- feedforward_errors_new: float32 [16, 2, 3072, 768], P('shard', 'section', 'tensor')
- attention_factor_new: float32 [4, 768, 32], P('section')
- feedforward_factor_new: float32 [2, 768, 32], P('section')
- attention_momentum_new: float32 [4, 768, 768], P('section', 'tensor', 'shard')
- feedforward_momentum_new: float32 [2, 3072, 768], P('section', 'tensor', 'shard')
- attention_master_new: float32 [4, 768, 768], P('section', 'tensor', 'shard')
- feedforward_master_new: float32 [2, 3072, 768], P('section', 'tensor', 'shard')
- attention_fresh: bfloat16 [4, 768, 768], P('section', 'tensor')
- feedforward_fresh: bfloat16 [2, 3072, 768], P('section', 'tensor')
- gain_momentum_new: float32 [2, 768], P('section', 'tensor')
- gain_weight_new: float32 [2, 768], P('section', 'tensor')
- bias_momentum_new: float32 [12, 32], P('tensor')
- bias_weight_new: float32 [12, 32], P('tensor')
All inputs are finite; a program needn't handle non-finite values.
Results may differ from a plain program's by a relative error of at most 0.0004.
Values may be sent and summed in bfloat16 or wider, within the bound.
A program may use at most 64 MiB of HBM per device.

v0:
```python
import jax
import jax.numpy as jnp
from jax import lax
from jax.sharding import PartitionSpec as P

NS_STEPS = 5
exact_mode = lax.Precision.HIGHEST
learn_rate = 0.05
decay_rate = 0.9


def inverse_root(gram_matrix):
    identity = jnp.broadcast_to(
        jnp.eye(gram_matrix.shape[-1], dtype=jnp.float32), gram_matrix.shape
    )
    frob_scale = jnp.sqrt(jnp.sum(gram_matrix * gram_matrix, axis=(-2, -1), keepdims=True)) + 1e-06
    converge = gram_matrix / frob_scale
    inverse = identity
    for turn_index in range(NS_STEPS):
        middle = 0.5 * (3.0 * identity - jnp.matmul(inverse, converge, precision=exact_mode))
        converge, inverse = (
            jnp.matmul(converge, middle, precision=exact_mode),
            jnp.matmul(middle, inverse, precision=exact_mode),
        )
    return inverse / jnp.sqrt(frob_scale)


def left_terms(merged, factor):
    return jnp.einsum("rmij,mjk->mik", merged, factor, precision=exact_mode)


def row_gram(matrix):
    return jnp.einsum("mik,mil->mkl", matrix, matrix, precision=exact_mode)


def right_terms(merged, ortho):
    return jnp.einsum("rmij,mik->mjk", merged, ortho, precision=exact_mode)


def per_device(
    attention_grads,
    feedforward_grads,
    attention_errors,
    feedforward_errors,
    attention_factor,
    feedforward_factor,
    attention_momentum,
    feedforward_momentum,
    attention_master,
    feedforward_master,
    gain_grads,
    bias_grads,
    gain_momentum,
    gain_weight,
    bias_momentum,
    bias_weight,
):
    replicas = lax.axis_size("shard")
    column_width = attention_master.shape[2]
    column_start = lax.axis_index("shard") * column_width
    attention_base = attention_master - learn_rate * decay_rate * attention_momentum
    feedforward_base = feedforward_master - learn_rate * decay_rate * feedforward_momentum
    attention_merged = attention_grads + attention_errors
    feedforward_merged = feedforward_grads + feedforward_errors
    attention_part = left_terms(attention_merged, attention_factor)
    feedforward_part = left_terms(feedforward_merged, feedforward_factor)
    attention_power, feedforward_power = lax.psum((attention_part, feedforward_part), "shard")
    attention_gram, feedforward_gram = lax.psum(
        (row_gram(attention_power), row_gram(feedforward_power)), "tensor"
    )
    attention_ortho = jnp.matmul(
        attention_power, inverse_root(attention_gram), precision=exact_mode
    )
    feedforward_ortho = jnp.matmul(
        feedforward_power, inverse_root(feedforward_gram), precision=exact_mode
    )
    attention_back, feedforward_back = lax.psum(
        (
            right_terms(attention_merged, attention_ortho),
            right_terms(feedforward_merged, feedforward_ortho),
        ),
        ("shard", "tensor"),
    )
    attention_back = attention_back / replicas
    feedforward_back = feedforward_back / replicas
    attention_approx = jnp.einsum(
        "mik,mjk->mij", attention_ortho, attention_back, precision=exact_mode
    )
    feedforward_approx = jnp.einsum(
        "mik,mjk->mij", feedforward_ortho, feedforward_back, precision=exact_mode
    )
    attention_errors_new = attention_merged - attention_approx[None]
    feedforward_errors_new = feedforward_merged - feedforward_approx[None]
    attention_factor_new = jnp.matmul(
        attention_back, inverse_root(row_gram(attention_back)), precision=exact_mode
    )
    feedforward_factor_new = jnp.matmul(
        feedforward_back, inverse_root(row_gram(feedforward_back)), precision=exact_mode
    )
    attention_slice = lax.dynamic_slice_in_dim(attention_approx, column_start, column_width, 2)
    feedforward_slice = lax.dynamic_slice_in_dim(feedforward_approx, column_start, column_width, 2)
    attention_momentum_new = decay_rate * attention_momentum + attention_slice
    feedforward_momentum_new = decay_rate * feedforward_momentum + feedforward_slice
    attention_master_new = attention_base - learn_rate * attention_slice
    feedforward_master_new = feedforward_base - learn_rate * feedforward_slice
    attention_fresh, feedforward_fresh = (
        lax.all_gather(attention_master_new.astype(jnp.bfloat16), "shard", axis=2, tiled=True),
        lax.all_gather(feedforward_master_new.astype(jnp.bfloat16), "shard", axis=2, tiled=True),
    )
    gain_total, bias_total = lax.psum((gain_grads[0], bias_grads[0]), "shard")
    gain_momentum_new = decay_rate * gain_momentum + gain_total / replicas
    gain_weight_new = gain_weight - learn_rate * gain_momentum_new
    bias_momentum_new = decay_rate * bias_momentum + bias_total / replicas
    bias_weight_new = bias_weight - learn_rate * bias_momentum_new
    return (
        attention_errors_new,
        feedforward_errors_new,
        attention_factor_new,
        feedforward_factor_new,
        attention_momentum_new,
        feedforward_momentum_new,
        attention_master_new,
        feedforward_master_new,
        attention_fresh,
        feedforward_fresh,
        gain_momentum_new,
        gain_weight_new,
        bias_momentum_new,
        bias_weight_new,
    )


def solution(mesh):
    placed = (
        P("shard", "section", "tensor", None),
        P("shard", "section", "tensor", None),
        P("shard", "section", "tensor", None),
        P("shard", "section", "tensor", None),
        P("section", None, None),
        P("section", None, None),
        P("section", "tensor", "shard"),
        P("section", "tensor", "shard"),
        P("section", "tensor", "shard"),
        P("section", "tensor", "shard"),
        P("shard", "section", "tensor"),
        P("shard", "tensor", None),
        P("section", "tensor"),
        P("section", "tensor"),
        P("tensor", None),
        P("tensor", None),
    )
    return jax.shard_map(
        per_device,
        mesh=mesh,
        in_specs=placed,
        out_specs=(
            P("shard", "section", "tensor", None),
            P("shard", "section", "tensor", None),
            P("section", None, None),
            P("section", None, None),
            P("section", "tensor", "shard"),
            P("section", "tensor", "shard"),
            P("section", "tensor", "shard"),
            P("section", "tensor", "shard"),
            P("section", "tensor", None),
            P("section", "tensor", None),
            P("section", "tensor"),
            P("section", "tensor"),
            P("tensor", None),
            P("tensor", None),
        ),
        check_vma=False,
    )
```

profile of v0, /device:TPU:0, one launch (start us, length us, event | category | flops | bytes accessed | tf_op | source)
XLA Modules:
  0.0 321.8 jit_solution(5114528691584657770)
XLA Ops:
  7.3 3.2 copy.39
  10.5 2.0 copy.40
  12.4 2.7 add.70
  15.1 2.2 fusion.2
  17.4 1.8 add.68
  19.2 1.0 copy-done.1
  20.2 1.2 fusion.6
  21.5 76.9 %all-reduce.1 = (f32[2,192,32]{1,2,0:T(8,128)S(1)}, f32[1,192]{1,0:T(1,128)S(1)}, f32[3,32]{1,0:T(4,128)S(1)}) all-reduce(f32[2,192,32]{1,2,0:T(8,128)S(1)} %fusion.6, f32[1,192]{1,0:T(1,128)S(1)} %bitcast.162, f32[3,32]{1,0:T(4,128)S(1)} %bitcast.161), channel_id=1, replica_groups=mesh['shard'=16,'tensor'=4,'section'=2] {'shard'}, use_global_device_ids=true, to_apply=%region_0.0 | all-reduce | flops 12576 | bytes 100608 | tf_op jit(solution)/shard_map/psum | solution.py:67
  98.6 3.7 %all-reduce.6.cloned.1.call-done = f32[768,32]{0,1:T(8,128)} async-done(((f32[768,32]{0,1:T(8,128)}), f32[768,32]{0,1:T(8,128)}) %all-reduce.6.cloned.1.call-update) | async-done | bytes 98320 | tf_op jit(solution)/shard_map/psum | solution.py:67
  102.3 1.3 convolution_bitcast_fusion.1
  103.6 17.4 %all-reduce.2 = (f32[2,32,32]{2,1,0:T(8,128)S(1)}, f32[1,32,32]{2,1,0:T(8,128)S(1)}) all-reduce(f32[2,32,32]{2,1,0:T(8,128)S(1)} %fusion.78, f32[1,32,32]{2,1,0:T(8,128)S(1)} %convolution_bitcast_fusion.1), channel_id=1, replica_groups=mesh['shard'=16,'tensor'=4,'section'=2] {'tensor'}, use_global_device_ids=true, to_apply=%region_1.0 | all-reduce | flops 3072 | bytes 24576 | tf_op jit(solution)/shard_map/psum | solution.py:68
  120.9 0.6 multiply_reduce_fusion.3
  124.2 0.2 fusion.20
  124.5 0.2 fusion.66
  126.7 0.3 fusion.92
  127.1 2.8 fusion.8
  130.1 0.2 convolution_divide_fusion.1
  130.3 0.2 fusion.85
  130.5 1.4 fusion.4
  132.0 0.2 all-gather.2.cloned.1.call-start
  132.2 0.6 multiply_subtract_fusion.2
  133.1 0.6 multiply_subtract_fusion.1
  133.7 121.8 %all-reduce.8.cloned.1.call-done = (f32[2,768,32]{1,2,0:T(8,128)}, f32[1,768,32]{1,2,0:T(8,128)}) async-done(((f32[2,768,32]{1,2,0:T(8,128)}, f32[1,768,32]{1,2,0:T(8,128)}), (f32[2,768,32]{1,2,0:T(8,128)}, f32[1,768,32]{1,2,0:T(8,128)})) %all-reduce.8.cloned.1.call-update) | async-done | bytes 294928 | tf_op jit(solution)/shard_map/psum | solution.py:77
  255.5 1.8 multiply_reduce_fusion.2
  259.8 1.4 multiply_reduce_fusion
  261.3 0.6 fusion.75
  261.8 0.2 fusion.15
  262.1 0.2 fusion.67
  262.7 0.8 fusion.94
  263.4 0.8 fusion.93
  264.2 4.5 %bitcast_subtract_fusion = (f32[1,1,768,768]{2,3,1,0:T(8,128)}, f32[768,768]{0,1:T(8,128)S(1)}) fusion(f32[1,1,768,768]{2,3,1,0:T(8,128)S(1)} %add.70, f32[768,32]{0,1:T(8,128)S(1)} %fusion.92, f32[1,768,32]{1,2,0:T(8,128)} %get-tuple-element.43), kind=kOutput, calls=%fused_computation | convolution fusion | flops 227106816 | bytes 7274496 | tf_op jit(solution)/shard_map/mik,mjk->mij/dot_general | solution.py:89
  268.7 2.6 bitcast_subtract_fusion.1
  271.3 0.8 fusion.76
  272.1 1.9 fusion.77
  274.0 0.7 copy.44
  274.9 0.8 convolution_divide_fusion.2
  275.6 22.5 %all_gather.6 = bf16[2,192,768]{1,0,2:T(2,128)(2,1)S(1)} all-gather(bf16[2,192,48]{1,0,2:T(2,128)(2,1)} %copy.44), channel_id=1, replica_groups=mesh['shard'=16,'tensor'=4,'section'=2] {'shard'}, dimensions={2}, use_global_device_ids=true | all-gather | bytes 626688 | tf_op jit(solution)/shard_map/all_gather | solution.py:107
  298.2 2.0 copy.45
  300.1 1.7 copy.48
  301.8 1.7 copy.46
  303.5 1.7 copy.47
  305.2 1.8 convolution_bitcast_fusion
  307.0 0.9 fusion.13
  308.0 0.9 fusion.96
  309.8 0.2 convolution_divide_fusion
  310.0 1.0 fusion.31
  311.0 1.9 all-gather.2.cloned.1.call-done
  312.9 2.4 copy.49
  (99 shorter events, 7.7 us)
Async XLA Ops:
  7.2 13.0 %copy-start = (f32[2,768,32]{1,2,0:T(8,128)S(1)}, f32[2,768,32]{1,2,0:T(8,128)}, u32[]{:S(2)}) copy-start(f32[2,768,32]{1,2,0:T(8,128)} %param.20) | copy-start | bytes 589828
  7.2 3.3 %copy-start.5 = (f32[1,1,768,768]{3,2,1,0:T(8,128)S(1)}, f32[1,1,768,768]{3,2,1,0:T(8,128)}, u32[]{:S(2)}) copy-start(f32[1,1,768,768]{3,2,1,0:T(8,128)} %param.19) | copy-start | bytes 7077892
  7.2 95.1 %all-reduce.6.cloned.1.call-start = ((), (), s32[]{:S(2)}) async-start(), calls=%async_computation | async-start | bytes 196608 | tf_op jit(solution)/shard_map/psum | solution.py:67
  12.4 2.7 copy-start.11
  15.1 2.3 copy-start.16
  17.3 238.1 %all-reduce.8.cloned.1.call-start = ((), (), s32[]{:S(2)}) async-start(), calls=%async_computation.2 | async-start | bytes 589824 | tf_op jit(solution)/shard_map/psum | solution.py:77
  17.4 4.0 %copy-start.17 = (f32[1,1,192]{2,1,0:T(1,128)S(1)}, f32[1,1,192]{2,1,0:T(1,128)}, u32[]{:S(2)}) copy-start(f32[1,1,192]{2,1,0:T(1,128)} %param.26) | copy-start | bytes 2308
  19.2 1.0 copy-start.1
  102.3 24.4 %copy-start.7 = (f32[768,32]{0,1:T(8,128)S(1)}, f32[768,32]{0,1:T(8,128)}, u32[]{:S(2)}) copy-start(f32[768,32]{0,1:T(8,128)} %all-reduce.6.cloned.1.call-done) | copy-start | bytes 294916
  124.1 6.4 %copy-start.2 = (f32[1,2,192,768]{3,2,1,0:T(8,128)S(1)}, f32[1,2,192,768]{3,2,1,0:T(8,128)}, u32[]{:S(2)}) copy-start(f32[1,2,192,768]{3,2,1,0:T(8,128)} %copy-done.1) | copy-start | bytes 3538948
  127.0 5.2 %copy-start.18 = (f32[1,192]{1,0:T(1,128)S(1)}, f32[1,192]{1,0:T(1,128)}, u32[]{:S(2)}) copy-start(f32[1,192]{1,0:T(1,128)} %param.29) | copy-start | bytes 2308
  127.0 5.2 %copy-start.19 = (f32[1,192]{1,0:T(1,128)S(1)}, f32[1,192]{1,0:T(1,128)}, u32[]{:S(2)}) copy-start(f32[1,192]{1,0:T(1,128)} %param.28) | copy-start | bytes 2308
  127.0 5.8 %copy-start.12 = (f32[2,192,48]{1,2,0:T(8,128)S(1)}, f32[2,192,48]{1,2,0:T(8,128)}, u32[]{:S(2)}) copy-start(f32[2,192,48]{1,2,0:T(8,128)} %param.22) | copy-start | bytes 221188
  127.0 5.9 %copy-start.13 = (f32[2,192,48]{1,2,0:T(8,128)S(1)}, f32[2,192,48]{1,2,0:T(8,128)}, u32[]{:S(2)}) copy-start(f32[2,192,48]{1,2,0:T(8,128)} %param.24) | copy-start | bytes 221188
  127.0 6.0 %copy-start.14 = (f32[3,32]{1,0:T(4,128)S(1)}, f32[3,32]{1,0:T(4,128)}, u32[]{:S(2)}) copy-start(f32[3,32]{1,0:T(4,128)} %param.31) | copy-start | bytes 1156
  127.1 6.0 %copy-start.15 = (f32[3,32]{1,0:T(4,128)S(1)}, f32[3,32]{1,0:T(4,128)}, u32[]{:S(2)}) copy-start(f32[3,32]{1,0:T(4,128)} %param.30) | copy-start | bytes 1156
  132.0 181.0 %all-gather.2.cloned.1.call-start = ((), (), s32[]{:S(2)}) async-start(), calls=%async_computation.1 | async-start | bytes 1253376 | tf_op jit(solution)/shard_map/all_gather | solution.py:108
  264.2 4.5 %copy-start.3 = (f32[1,2,192,768]{3,2,1,0:T(8,128)S(1)}, f32[1,2,192,768]{3,2,1,0:T(8,128)}, u32[]{:S(2)}) copy-start(f32[1,2,192,768]{3,2,1,0:T(8,128)} %copy-done.1) | copy-start | bytes 3538948
  264.2 4.5 %copy-start.6 = (f32[2,768,32]{1,2,0:T(8,128)S(1)}, f32[2,768,32]{1,2,0:T(8,128)}, u32[]{:S(2)}) copy-start(f32[2,768,32]{1,2,0:T(8,128)} %get-tuple-element.42) | copy-start | bytes 589828
  268.7 2.6 copy-start.9
  268.7 2.6 copy-start.10
  271.3 26.9 %copy-start.4 = (f32[1,1,768,768]{2,3,1,0:T(8,128)S(1)}, f32[1,1,768,768]{2,3,1,0:T(8,128)}, u32[]{:S(2)}) copy-start(f32[1,1,768,768]{2,3,1,0:T(8,128)} %get-tuple-element.65) | copy-start | bytes 7077892
  300.1 8.8 %copy-start.8 = (f32[2,32,32]{2,1,0:T(8,128)S(1)}, f32[2,32,32]{2,1,0:T(8,128)}, u32[]{:S(2)}) copy-start(f32[2,32,32]{2,1,0:T(8,128)} %fusion.93) | copy-start | bytes 24580
  300.1 9.6 %copy-start.20 = (f32[2]{0:T(128)S(1)}, f32[2]{0:T(128)}, u32[]{:S(2)}) copy-start(f32[2]{0:T(128)} %get-tuple-element.59) | copy-start | bytes 28
Sparse Core Ops, SparseCore 0:
  17.5 84.7 all-reduce.5
  132.1 123.3 all-reduce.7
  272.2 40.6 all-gather.1
where the time goes:
time: 322 us
  waiting for transfers between devices  128 us (40%)
  blocking collectives  117 us (36%)
  matrix products  35.2 us (11%)
  local copies, waits for them, and re-layouts  16.6 us (5%)
  between operations  15.8 us (5%)
  other arithmetic  9.61 us (3%)
    psum x1, waiting for transfers between devices, per_device(): lax.psum((right_terms(attention_merged, attention_ortho), right_terms(fee...  122 us
    psum x1, blocking collectives, per_device(): lax.psum((attention_part, feedforward_part), 'shard')  76.9 us
    all_gather x1, blocking collectives, per_device(): lax.all_gather(attention_master_new.astype(jnp.bfloat16), 'shard', axis=2...  22.5 us
    psum x1, blocking collectives, per_device(): lax.psum((row_gram(attention_power), row_gram(feedforward_power)), 'tensor')  17.4 us
    unnamed x52, local copies, waits for them, and re-layouts  15.9 us
  transfers between devices with their start and end apart: 3, of which 3 were waited for; matrix products, arithmetic and copies ran while one was open for 6% of the time, Pallas kernels for 0%

commit v1 on v0

--- a/solution.py
+++ b/solution.py
@@ -2,6 +2,7 @@
 import jax.numpy as jnp
 from jax import lax
 from jax.sharding import PartitionSpec as P
+from jax.lax import all_to_all, axis_size
 
 NS_STEPS = 5
 exact_mode = lax.Precision.HIGHEST
@@ -55,6 +56,18 @@
     bias_momentum,
     bias_weight,
 ):
+
+    def part_vectors(xx):
+        return jnp.concatenate(
+            all_to_all(
+                jnp.stack(axis_size("shard") * [xx], axis=0),
+                axis_name="shard",
+                split_axis=0,
+                concat_axis=0,
+            ),
+            axis=2,
+        )
+
     replicas = lax.axis_size("shard")
     column_width = attention_master.shape[2]
     column_start = lax.axis_index("shard") * column_width
@@ -104,7 +117,7 @@
     attention_master_new = attention_base - learn_rate * attention_slice
     feedforward_master_new = feedforward_base - learn_rate * feedforward_slice
     attention_fresh, feedforward_fresh = (
-        lax.all_gather(attention_master_new.astype(jnp.bfloat16), "shard", axis=2, tiled=True),
+        part_vectors(attention_master_new.astype(jnp.bfloat16)),
         lax.all_gather(feedforward_master_new.astype(jnp.bfloat16), "shard", axis=2, tiled=True),
     )
     gain_total, bias_total = lax.psum((gain_grads[0], bias_grads[0]), "shard")

time: 322 us -> 327 us (1.016)
  blocking collectives: 117 us -> 94.3 us
  waiting for transfers between devices: 128 us -> 145 us
  starting transfers between devices: 0.3 us -> 4.64 us
  matrix products: 35.2 us -> 39.2 us
    all_gather x1 -> x0, blocking collectives: 22.5 us -> none  [per_device(): lax.all_gather(attention_master_new.astype(jnp.bfloat16), 'shard', axis=2...]
    all_gather x1, waiting for transfers between devices: 1.95 us -> 20.2 us  [per_device(): lax.all_gather(feedforward_master_new.astype(jnp.bfloat16), 'shard', axis...]
    all_to_all x0 -> x1, starting transfers between devices: none -> 4.33 us  [part_vectors(): all_to_all(jnp.stack(axis_size('shard') * [xx], axis=0), axis_name='shard...]
    unnamed x52 -> x46, local copies, waits for them, and re-layouts: 15.9 us -> 16.1 us
  transfers between devices with their start and end apart: 3 -> 4, of which waited for: 3 -> 3; matrix products, arithmetic and copies ran while one was open for 6% -> 7% of each run, Pallas kernels for 0% -> 0%
where the time goes in v1:
time: 327 us; the launch traced here: 326 us
  waiting for transfers between devices  145 us (44%)
  blocking collectives  94.3 us (29%)
  matrix products  39.2 us (12%)
  local copies, waits for them, and re-layouts  17.2 us (5%)
  between operations  15.8 us (5%)
  other arithmetic  9.65 us (3%)
  starting transfers between devices  4.64 us (1%)
    psum x1, waiting for transfers between devices, per_device(): lax.psum((right_terms(attention_merged, attention_ortho), right_terms(fee...  121 us
    psum x1, blocking collectives, per_device(): lax.psum((attention_part, feedforward_part), 'shard')  76.9 us
    all_gather x1, waiting for transfers between devices, per_device(): lax.all_gather(feedforward_master_new.astype(jnp.bfloat16), 'shard', axis...  20.2 us
    psum x1, blocking collectives, per_device(): lax.psum((row_gram(attention_power), row_gram(feedforward_power)), 'tensor')  17.4 us
    unnamed x46, local copies, waits for them, and re-layouts  16.1 us
    dot_general x20, matrix products, inverse_root(): jnp.matmul(middle, inverse, precision=exact_mode)  7.05 us
  transfers between devices with their start and end apart: 4, of which 3 were waited for; matrix products, arithmetic and copies ran while one was open for 7% of the time, Pallas kernels for 0%

profile of v1, /device:TPU:0, one launch (start us, length us, event | category | flops | bytes accessed | tf_op | source)
XLA Modules:
  0.0 325.7 jit_solution(17155772035560129326)
XLA Ops:
  7.3 3.2 copy.51
  10.5 2.0 copy.52
  12.4 2.7 add.70
  15.1 2.2 fusion.2
  17.4 1.8 add.68
  19.2 1.0 copy-done.1
  20.2 1.2 fusion.6
  21.5 76.9 %all-reduce.1 = (f32[2,192,32]{1,2,0:T(8,128)S(1)}, f32[1,192]{1,0:T(1,128)S(1)}, f32[3,32]{1,0:T(4,128)S(1)}) all-reduce(f32[2,192,32]{1,2,0:T(8,128)S(1)} %fusion.6, f32[1,192]{1,0:T(1,128)S(1)} %bitcast.166, f32[3,32]{1,0:T(4,128)S(1)} %bitcast.165), channel_id=1, replica_groups=mesh['shard'=16,'tensor'=4,'section'=2] {'shard'}, use_global_device_ids=true, to_apply=%region_0.0 | all-reduce | flops 12576 | bytes 100608 | tf_op jit(solution)/shard_map/psum | solution.py:80
  98.6 3.7 %all-reduce.6.cloned.1.call-done = f32[768,32]{0,1:T(8,128)} async-done(((f32[768,32]{0,1:T(8,128)}), f32[768,32]{0,1:T(8,128)}) %all-reduce.6.cloned.1.call-update) | async-done | bytes 98320 | tf_op jit(solution)/shard_map/psum | solution.py:80
  102.3 1.3 convolution_bitcast_fusion.1
  103.6 17.4 %all-reduce.2 = (f32[2,32,32]{2,1,0:T(8,128)S(1)}, f32[1,32,32]{2,1,0:T(8,128)S(1)}) all-reduce(f32[2,32,32]{2,1,0:T(8,128)S(1)} %fusion.78, f32[1,32,32]{2,1,0:T(8,128)S(1)} %convolution_bitcast_fusion.1), channel_id=1, replica_groups=mesh['shard'=16,'tensor'=4,'section'=2] {'tensor'}, use_global_device_ids=true, to_apply=%region_1.0 | all-reduce | flops 3072 | bytes 24576 | tf_op jit(solution)/shard_map/psum | solution.py:81
  120.9 0.6 multiply_reduce_fusion.3
  124.2 0.2 fusion.20
  126.7 0.3 fusion.92
  127.1 2.8 fusion.8
  130.2 0.3 fusion.85
  130.5 1.4 fusion.4
  132.2 0.6 multiply_subtract_fusion.2
  132.9 1.0 copy.56
  133.9 0.6 multiply_subtract_fusion.1
  134.5 120.9 %all-reduce.8.cloned.1.call-done = (f32[2,768,32]{1,2,0:T(8,128)}, f32[1,768,32]{1,2,0:T(8,128)}) async-done(((f32[2,768,32]{1,2,0:T(8,128)}, f32[1,768,32]{1,2,0:T(8,128)}), (f32[2,768,32]{1,2,0:T(8,128)}, f32[1,768,32]{1,2,0:T(8,128)})) %all-reduce.8.cloned.1.call-update) | async-done | bytes 294928 | tf_op jit(solution)/shard_map/psum | solution.py:90
  255.5 1.8 multiply_reduce_fusion.2
  259.5 0.8 fusion.104
  260.2 0.7 fusion.103
  261.0 1.4 multiply_reduce_fusion
  262.4 0.6 fusion.75
  263.9 0.8 fusion.94
  264.6 0.8 fusion.93
  265.4 4.5 %bitcast_subtract_fusion = (f32[1,1,768,768]{2,3,1,0:T(8,128)}, f32[768,768]{0,1:T(8,128)S(1)}) fusion(f32[1,1,768,768]{2,3,1,0:T(8,128)S(1)} %add.70, f32[768,32]{0,1:T(8,128)S(1)} %fusion.92, f32[1,768,32]{1,2,0:T(8,128)} %get-tuple-element.57), kind=kOutput, calls=%fused_computation | convolution fusion | flops 227106816 | bytes 7274496 | tf_op jit(solution)/shard_map/mik,mjk->mij/dot_general | solution.py:102
  270.0 2.6 bitcast_subtract_fusion.1
  272.5 0.8 fusion.76
  273.3 1.9 fusion.77
  275.3 1.0 stack.2
  276.3 4.3 %all-to-all-start = ((bf16[16,2,192,48]{2,3,1,0:T(8,128)(2,1)}), bf16[16,2,192,48]{2,3,1,0:T(8,128)(2,1)S(1)}, u32[]{:S(2)}, u32[]{:S(2)}) async-start(bf16[16,2,192,48]{2,3,1,0:T(8,128)(2,1)} %stack.2), calls=%async_computation | async-start | bytes 1572864 | tf_op jit(solution)/shard_map/all_to_all | solution.py:62
  280.6 0.9 fusion.21
  281.5 1.5 convolution_divide_fusion.2
  283.0 1.9 copy.59
  284.9 1.7 copy.60
  286.6 1.7 copy.61
  288.3 0.9 fusion.13
  289.2 0.9 fusion.96
  290.1 0.9 fusion.95
  291.7 1.8 convolution_bitcast_fusion
  293.6 0.8 convolution_divide_fusion
  294.4 1.0 fusion.31
  295.5 1.1 copy.62
  296.6 20.2 %all-gather.2.cloned.1.call-done = bf16[1,768,768]{1,2,0:T(8,128)(2,1)} async-done(((bf16[1,768,48]{1,2,0:T(8,128)(2,1)}), bf16[1,768,768]{1,2,0:T(8,128)(2,1)}) %all-gather.2.cloned.1.call-update) | async-done | bytes 1179664 | tf_op jit(solution)/shard_map/all_gather | solution.py:121
  316.8 2.4 copy.63
  (96 shorter events, 8.2 us)
Async XLA Ops:
  7.2 13.1 %copy-start = (f32[2,768,32]{1,2,0:T(8,128)S(1)}, f32[2,768,32]{1,2,0:T(8,128)}, u32[]{:S(2)}) copy-start(f32[2,768,32]{1,2,0:T(8,128)} %param.20) | copy-start | bytes 589828
  7.2 3.3 %copy-start.5 = (f32[1,1,768,768]{3,2,1,0:T(8,128)S(1)}, f32[1,1,768,768]{3,2,1,0:T(8,128)}, u32[]{:S(2)}) copy-start(f32[1,1,768,768]{3,2,1,0:T(8,128)} %param.19) | copy-start | bytes 7077892
  7.2 95.1 %all-reduce.6.cloned.1.call-start = ((), (), s32[]{:S(2)}) async-start(), calls=%async_computation.1 | async-start | bytes 196608 | tf_op jit(solution)/shard_map/psum | solution.py:80
  12.4 2.7 copy-start.10
  15.1 2.3 copy-start.14
  17.3 238.1 %all-reduce.8.cloned.1.call-start = ((), (), s32[]{:S(2)}) async-start(), calls=%async_computation.3 | async-start | bytes 589824 | tf_op jit(solution)/shard_map/psum | solution.py:90
  17.4 4.0 %copy-start.15 = (f32[1,1,192]{2,1,0:T(1,128)S(1)}, f32[1,1,192]{2,1,0:T(1,128)}, u32[]{:S(2)}) copy-start(f32[1,1,192]{2,1,0:T(1,128)} %param.26) | copy-start | bytes 2308
  19.2 1.0 copy-start.1
  102.3 24.4 %copy-start.7 = (f32[768,32]{0,1:T(8,128)S(1)}, f32[768,32]{0,1:T(8,128)}, u32[]{:S(2)}) copy-start(f32[768,32]{0,1:T(8,128)} %all-reduce.6.cloned.1.call-done) | copy-start | bytes 294916
  124.1 6.4 %copy-start.2 = (f32[1,2,192,768]{3,2,1,0:T(8,128)S(1)}, f32[1,2,192,768]{3,2,1,0:T(8,128)}, u32[]{:S(2)}) copy-start(f32[1,2,192,768]{3,2,1,0:T(8,128)} %copy-done.1) | copy-start | bytes 3538948
  127.0 5.2 %copy-start.16 = (f32[1,192]{1,0:T(1,128)S(1)}, f32[1,192]{1,0:T(1,128)}, u32[]{:S(2)}) copy-start(f32[1,192]{1,0:T(1,128)} %param.29) | copy-start | bytes 2308
  127.0 5.2 %copy-start.17 = (f32[1,192]{1,0:T(1,128)S(1)}, f32[1,192]{1,0:T(1,128)}, u32[]{:S(2)}) copy-start(f32[1,192]{1,0:T(1,128)} %param.28) | copy-start | bytes 2308
  127.0 5.8 %copy-start.11 = (f32[2,192,48]{1,2,0:T(8,128)S(1)}, f32[2,192,48]{1,2,0:T(8,128)}, u32[]{:S(2)}) copy-start(f32[2,192,48]{1,2,0:T(8,128)} %param.22) | copy-start | bytes 221188
  127.0 6.9 %copy-start.12 = (f32[3,32]{1,0:T(4,128)S(1)}, f32[3,32]{1,0:T(4,128)}, u32[]{:S(2)}) copy-start(f32[3,32]{1,0:T(4,128)} %param.31) | copy-start | bytes 1156
  127.0 6.9 %copy-start.13 = (f32[3,32]{1,0:T(4,128)S(1)}, f32[3,32]{1,0:T(4,128)}, u32[]{:S(2)}) copy-start(f32[3,32]{1,0:T(4,128)} %param.30) | copy-start | bytes 1156
  132.0 184.8 %all-gather.2.cloned.1.call-start = ((), (), s32[]{:S(2)}) async-start(), calls=%async_computation.2 | async-start | bytes 1253376 | tf_op jit(solution)/shard_map/all_gather | solution.py:121
  265.4 4.5 %copy-start.3 = (f32[1,2,192,768]{3,2,1,0:T(8,128)S(1)}, f32[1,2,192,768]{3,2,1,0:T(8,128)}, u32[]{:S(2)}) copy-start(f32[1,2,192,768]{3,2,1,0:T(8,128)} %copy-done.1) | copy-start | bytes 3538948
  265.4 4.5 %copy-start.6 = (f32[2,768,32]{1,2,0:T(8,128)S(1)}, f32[2,768,32]{1,2,0:T(8,128)}, u32[]{:S(2)}) copy-start(f32[2,768,32]{1,2,0:T(8,128)} %get-tuple-element.56) | copy-start | bytes 589828
  269.9 2.6 copy-start.8
  269.9 2.6 copy-start.9
  272.5 10.5 %copy-start.4 = (f32[1,1,768,768]{2,3,1,0:T(8,128)S(1)}, f32[1,1,768,768]{2,3,1,0:T(8,128)}, u32[]{:S(2)}) copy-start(f32[1,1,768,768]{2,3,1,0:T(8,128)} %get-tuple-element.79) | copy-start | bytes 7077892
  276.3 19.2 %all-to-all-start = ((bf16[16,2,192,48]{2,3,1,0:T(8,128)(2,1)}), bf16[16,2,192,48]{2,3,1,0:T(8,128)(2,1)S(1)}, u32[]{:S(2)}, u32[]{:S(2)}) async-start(bf16[16,2,192,48]{2,3,1,0:T(8,128)(2,1)} %stack.2), calls=%async_computation | async-start | bytes 1572864 | tf_op jit(solution)/shard_map/all_to_all | solution.py:62
Sparse Core Ops, SparseCore 0:
  17.5 84.7 all-reduce.5
  132.1 123.3 all-reduce.7
  273.4 43.3 all-gather.1
